TPU v7x, 128 devices: a whole 4x4x4 slice. The times are simulated.
128 devices in a mesh: req: 32 (over y, z, core), seq: 4 (over x).
Axes of the slice: x: 4, y: 4, z: 4, core: 2. Of those that a mesh axis runs over, the one named last changes fastest.
Arguments:
- hidden_in: bfloat16 [32, 1024, 1792], P('req', 'seq'), may hold values from -6 to 6
- lengths: int32 [32], P('req'), may hold values from 1 to 1024, 16384 in all
- log_decay: float32 [32, 1024, 8], P('req', 'seq'), may hold values from -1 to 0
- mix_gain: float32 [1792], replicated, may hold values from 0.1 to 1.9
- conv_weight: float32 [3, 1792], replicated, may hold values from -3 to 3
- query_weight: bfloat16 [1792, 128], replicated, may hold values from -0.375 to 0.375
- key_weight: bfloat16 [1792, 128], replicated, may hold values from -0.375 to 0.375
- value_weight: bfloat16 [1792, 896], replicated, may hold values from -0.125 to 0.125
- out_weight: bfloat16 [896, 1792], replicated, may hold values from -0.1875 to 0.1875
- mlp_gain: float32 [1792], replicated, may hold values from 0.1 to 1.9
- gate_weight: bfloat16 [1792, 1792], P(None, 'req'), may hold values from -0.125 to 0.125
- up_weight: bfloat16 [1792, 1792], P(None, 'req'), may hold values from -0.125 to 0.125
- down_weight: bfloat16 [1792, 1792], P(None, 'req'), may hold values from -0.125 to 0.125
Outputs:
- layer_out: bfloat16 [32, 1024, 1792], P('req', 'seq')
- end_states: float32 [32, 4, 273, 896], P('req', 'seq')
- end_norms: float32 [32, 4, 273, 8], P('req', 'seq')
Inputs may be any that keep to these rules, and one draw needn't show every extreme that they name: Each prompt has at least one token; the lengths sum to 16384 and the longest fills all 1024 slots.
All inputs are finite; a program needn't handle non-finite values. No bound on the sum of `lengths` on one device may be relied on, other than what follows from the above.
Results may differ from a plain program's by a relative error of at most 0.0085.
Values may be sent and summed in bfloat16 or wider, within the bound.
A program may use at most 128 MiB of HBM per device.

v0:
```python
import jax
import jax.numpy as jnp
from jax import lax
from jax.sharding import PartitionSpec as P


def from_behind(array, axis, by):
    count = lax.axis_size(axis)
    pairs = [(i, i + by) for i in range(count) if 0 <= i + by < count]
    return lax.ppermute(array, axis, pairs)


def entering(array, axis, combine, identity):
    count, here = (lax.axis_size(axis), lax.axis_index(axis))
    everything = jax.tree.map(
        lambda part, kind: lax.all_gather(part.astype(kind), axis),
        array,
        (jnp.bfloat16, jnp.bfloat16, jnp.bfloat16),
    )
    start = jax.tree.map(
        lambda part, zero: jnp.broadcast_to(jnp.asarray(zero, part.dtype), part.shape),
        array,
        identity,
    )

    def hop(k, before):
        reached = k < here
        new = combine(
            before, jax.tree.map(lambda part, own: part[k].astype(own.dtype), everything, array)
        )
        return jax.tree.map(lambda a, b: jnp.where(reached, a, b), new, before)

    return lax.fori_loop(0, count, hop, start)


def features(vectors):
    constant = jnp.ones(vectors.shape[:-1] + (1,), jnp.float32)
    width = vectors.shape[-1]
    squares = (vectors[..., :, None] * vectors[..., None, :]).reshape(
        vectors.shape[:-1] + (width * width,)
    )
    return jnp.concatenate([constant, vectors, squares * 0.5**0.5], axis=-1)


def block_step(carry, inputs):
    memory, key_sum = carry
    query_blk, key_blk, value_blk, value_half, decay_rate, valid_mask = inputs
    highest = lax.Precision.HIGHEST
    cumulative = jnp.cumsum(decay_rate, axis=0)
    scores = jnp.einsum("thi,uhi->htu", query_blk, key_blk, precision=highest)
    kernel = 1.0 + scores + 0.5 * scores * scores
    gap_log = cumulative.T[:, :, None] - cumulative.T[:, None, :]
    block_len = decay_rate.shape[0]
    causal = jnp.arange(block_len)[:, None] >= jnp.arange(block_len)[None, :]
    weights = (
        jnp.where(causal[None], jnp.exp(jnp.minimum(gap_log, 0.0)), 0.0)
        * kernel
        * valid_mask[None, None, :]
    )
    numerator = jnp.einsum(
        "htu,uhv->thv", weights.astype(jnp.bfloat16), value_half, preferred_element_type=jnp.float32
    )
    denominator = jnp.sum(weights, axis=2).T
    query_feat = features(query_blk)
    key_feat = features(key_blk) * valid_mask[:, None, None]
    growth = jnp.exp(cumulative)
    numerator = (
        numerator
        + jnp.einsum("thf,fhv->thv", query_feat, memory, precision=highest) * growth[:, :, None]
    )
    denominator = (
        denominator + jnp.einsum("thf,fh->th", query_feat, key_sum, precision=highest) * growth
    )
    closing = cumulative[-1]
    fading = jnp.exp(closing[None, :] - cumulative)
    faded_keys = key_feat * fading[:, :, None]
    memory = memory * jnp.exp(closing)[None, :, None] + jnp.einsum(
        "uhf,uhv->fhv", faded_keys, value_blk, precision=highest
    )
    key_sum = key_sum * jnp.exp(closing)[None, :] + jnp.sum(faded_keys, axis=0).T
    return ((memory, key_sum), (numerator, denominator))


def span_attention(
    query_f32, key_f32, value_f32, value_half, decay_rate, valid_mask, memory, key_sum, block_len
):
    span = query_f32.shape[0]
    blocks = span // block_len

    def split(array):
        return array.reshape((blocks, block_len) + array.shape[1:])

    carry, outputs = lax.scan(
        block_step,
        (memory, key_sum),
        (
            split(query_f32),
            split(key_f32),
            split(value_f32),
            split(value_half),
            split(decay_rate),
            split(valid_mask),
        ),
    )
    numerator = outputs[0].reshape((span,) + outputs[0].shape[2:])
    denominator = outputs[1].reshape((span,) + outputs[1].shape[2:])
    return (carry[0], carry[1], numerator, denominator)


def rms_scale(rows, gain):
    rows_f32 = rows.astype(jnp.float32)
    factor = lax.rsqrt(jnp.mean(rows_f32 * rows_f32, axis=-1, keepdims=True) + 1e-05)
    return (rows_f32 * factor * gain).astype(jnp.bfloat16)


def feed_forward(row_data, valid_count, gate_weight, up_weight, down_weight):
    row_total = row_data.shape[0]
    block_len = min(256, row_total)
    live_blocks = (valid_count + block_len - 1) // block_len
    initial = jnp.zeros((row_total, row_data.shape[1]), jnp.float32)
    gate_piece = lax.all_gather(gate_weight, "req", axis=1, tiled=True)
    up_piece = lax.all_gather(up_weight, "req", axis=1, tiled=True)
    down_piece = lax.all_gather(down_weight, "req", axis=1, tiled=True)

    def add_block(index, accumulated):
        gate_act = jnp.dot(row_data, gate_piece, preferred_element_type=jnp.float32)
        up_act = jnp.dot(row_data, up_piece, preferred_element_type=jnp.float32)
        hidden_units = (jax.nn.silu(gate_act) * up_act).astype(jnp.bfloat16)
        increment = lax.dot_general(
            hidden_units, down_piece, (((1,), (1,)), ((), ())), preferred_element_type=jnp.float32
        )
        return accumulated + increment

    return lax.fori_loop(0, live_blocks, add_block, initial)


def finish_rows(mixed_rows, valid_mask, mlp_gain, gate_weight, up_weight, down_weight):
    mlp_in = rms_scale(mixed_rows, mlp_gain)
    valid_count = jnp.sum(valid_mask).astype(jnp.int32)
    ffn_out = feed_forward(mlp_in, valid_count, gate_weight, up_weight, down_weight)
    return ((mixed_rows.astype(jnp.float32) + ffn_out) * valid_mask[:, None]).astype(jnp.bfloat16)


def local(
    hidden_in,
    lengths,
    log_decay,
    mix_gain,
    conv_weight,
    query_weight,
    key_weight,
    value_weight,
    out_weight,
    mlp_gain,
    gate_weight,
    up_weight,
    down_weight,
):
    local_len = hidden_in.shape[1]
    rows_in = hidden_in[0]
    decays = log_decay[0]
    head_count = log_decay.shape[2]
    value_len = value_weight.shape[1] // head_count
    feat_in = query_weight.shape[1] // head_count
    feat_len = 1 + feat_in + feat_in * feat_in
    tap_count = conv_weight.shape[0]
    block_len = min(256, local_len)
    feature_scale = feat_in ** (-0.25)
    token_positions = lax.axis_index("seq") * local_len + jnp.arange(local_len, dtype=jnp.int32)
    valid_mask = (token_positions < lengths[0]).astype(jnp.float32)
    normed = rms_scale(rows_in, mix_gain)
    edge_rows = from_behind(normed[local_len - (tap_count - 1) :], "seq", 1)
    extended = jnp.concatenate([edge_rows, normed], axis=0)
    convolved = jnp.zeros(normed.shape, jnp.float32)
    for tap in range(tap_count):
        convolved = convolved + conv_weight[tap][None, :] * extended[
            tap_count - 1 - tap : tap_count - 1 - tap + local_len
        ].astype(jnp.float32)
    gated_rows = (convolved * jax.nn.sigmoid(normed.astype(jnp.float32))).astype(jnp.bfloat16)
    queries = (
        jnp.dot(gated_rows, query_weight, preferred_element_type=jnp.float32) * feature_scale
    ).astype(jnp.bfloat16)
    key_rows = (
        jnp.dot(gated_rows, key_weight, preferred_element_type=jnp.float32) * feature_scale
    ).astype(jnp.bfloat16)
    values = jnp.dot(gated_rows, value_weight, preferred_element_type=jnp.float32).astype(
        jnp.bfloat16
    )
    query_f32 = queries.astype(jnp.float32).reshape(local_len, head_count, feat_in)
    key_f32 = key_rows.astype(jnp.float32).reshape(local_len, head_count, feat_in)
    value_half = values.reshape(local_len, head_count, value_len)
    value_f32 = value_half.astype(jnp.float32)
    decay_rate = jnp.where(valid_mask[:, None] > 0, decays, 0.0)
    empty_memory = jnp.zeros((feat_len, head_count, value_len), jnp.float32)
    empty_keys = jnp.zeros((feat_len, head_count), jnp.float32)
    memory, key_sum, numerator, denominator = span_attention(
        query_f32,
        key_f32,
        value_f32,
        value_half,
        decay_rate,
        valid_mask,
        empty_memory,
        empty_keys,
        block_len,
    )
    span_decay = jnp.sum(decay_rate, axis=0)
    flat_memory = memory.reshape(feat_len, head_count * value_len)

    def merge_states(earlier, later):
        factor = jnp.exp(later[0])
        return (
            earlier[0] + later[0],
            earlier[1] * jnp.repeat(factor, value_len)[None, :] + later[1],
            earlier[2] * factor[None, :] + later[2],
        )

    neutral = (jnp.zeros_like(span_decay), jnp.zeros_like(flat_memory), jnp.zeros_like(key_sum))
    carried = entering((span_decay, flat_memory, key_sum), "seq", merge_states, neutral)
    prior_memory = carried[1]
    prior_keys = carried[2]
    highest = lax.Precision.HIGHEST
    growth = jnp.exp(jnp.cumsum(decay_rate, axis=0))
    query_feat = features(query_f32)
    numerator = (
        numerator
        + jnp.einsum(
            "thf,fhv->thv",
            query_feat,
            prior_memory.reshape(feat_len, head_count, value_len),
            precision=highest,
        )
        * growth[:, :, None]
    )
    denominator = (
        denominator + jnp.einsum("thf,fh->th", query_feat, prior_keys, precision=highest) * growth
    )
    attended = (
        (numerator / denominator[:, :, None])
        .reshape(local_len, head_count * value_len)
        .astype(jnp.bfloat16)
    )
    mixed_rows = (
        rows_in.astype(jnp.float32)
        + jnp.dot(attended, out_weight, preferred_element_type=jnp.float32)
    ).astype(jnp.bfloat16)
    span_factor = jnp.exp(span_decay)
    end_state = prior_memory * jnp.repeat(span_factor, value_len)[None, :] + flat_memory
    end_norm = prior_keys * span_factor[None, :] + key_sum
    result = finish_rows(mixed_rows, valid_mask, mlp_gain, gate_weight, up_weight, down_weight)
    return (result[None], end_state[None, None], end_norm[None, None])


def solution(mesh):
    return jax.shard_map(
        local,
        mesh=mesh,
        in_specs=(
            P("req", "seq", None),
            P("req"),
            P("req", "seq", None),
            P(),
            P(),
            P(),
            P(),
            P(),
            P(),
            P(),
            P(None, "req"),
            P(None, "req"),
            P(None, "req"),
        ),
        out_specs=(P("req", "seq", None), P("req", "seq", None, None), P("req", "seq", None, None)),
        check_vma=False,
    )
```

profile of v0, /device:TPU:1, one launch (start us, length us, event | category | flops | bytes accessed | tf_op | source)
XLA Modules:
  0.0 244.9 jit_solution(10854756418598120270)
XLA Ops:
  7.2 1.6 fusion.23
  8.8 1.5 fusion.25
  10.3 0.9 copy-done.5
  11.3 3.9 %collective-permute-start = (bf16[2,1792]{1,0:T(2,128)(2,1)S(1)}, bf16[2,1792]{1,0:T(2,128)(2,1)S(1)}, u32[]{:S(2)}, u32[]{:S(2)}) collective-permute-start(bf16[2,1792]{1,0:T(2,128)(2,1)S(1)} %slice.39), channel_id=1, source_target_pairs={{0,1},{1,2},{2,3},{4,5},{5,6},{6,7},{8,9},{9,10},{10,11},{12,13},{... | collective-permute-start | bytes 21512 | tf_op jit(solution)/shard_map/ppermute | solution.py:10
  16.0 0.6 reduce-window.12
  16.9 0.7 multiply_reduce_fusion
  17.7 3.0 %fusion.14 = bf16[256,1792]{1,0:T(8,128)(2,1)S(1)} fusion(bf16[256,1792]{1,0:T(8,128)(2,1)} %copy-done.5, bf16[2,1792]{1,0:T(2,128)(2,1)S(1)} %collective-permute-done, f32[1792]{0:T(1024)S(1)} %get-tuple-element.331, f32[1792]{0:T(1024)S(1)} %get-tuple-element.332, f32[1792]{0:T(1024)S(1)} %get-tuple-element.330), kind=kLoop, calls=%fused_computation.31 | loop fusion | flops 8716288 | bytes 1863680 | tf_op jit(solution)/shard_map/convert_element_type | solution.py:179
  21.2 1.6 multiply_multiply_fusion.1
  22.8 0.9 copy-done.25
  23.7 1.9 convolution_convert_fusion
  25.6 2.0 copy.43
  27.6 3.3 %fusion.27 = f32[8,112,273]{1,2,0:T(8,128)S(1)} fusion(bf16[256,8,112]{0,2,1:T(8,128)(2,1)} %bitcast.123, f32[256,8,256]{0,2,1:T(8,128)} %bitcast.121, f32[256,8,16]{0,2,1:T(8,128)S(1)} %get-tuple-element.365, f32[273]{0:T(512)S(1)} %pad.3.clone, f32[256,8]{0,1:T(8,128)S(1)} %subtract_exponential_fusion, f32[256]{0:T(256)S(1)} %get-tuple-element.371), kind=kOutput, calls=%fused_computation.44 | convolution fusion | flops 753672192 | bytes 3675716 | tf_op jit(solution)/shard_map/while/body/eval_jaxpr/uhf,uhv->fhv/dot_general | solution.py:77
  31.0 1.5 fusion.66
  32.4 2.4 convert_element_type.161
  34.9 0.7 all-gather.10.cloned.1.call-update
  35.6 0.7 all-gather.12.cloned.1.call-update
  36.9 0.6 fusion.65
  38.2 0.6 dynamic-slice.2
  39.7 7.2 %all-reduce = bf16[32]{0:T(256)(128)(2,1)S(1)} all-reduce(bf16[32]{0:T(256)(128)(2,1)S(1)} %dynamic-update-slice), channel_id=2, replica_groups=mesh['req'=32,'seq'=4] {'seq'}, use_global_device_ids=true, to_apply=%add | all-reduce | flops 32 | bytes 128
  46.9 0.6 reshape.203
  47.7 0.7 add_bitcast_fusion.2
  48.4 2.7 %reshape.199 = f32[273,896]{1,0:T(8,128)} reshape(f32[273,8,112]{2,1,0:T(8,128)} %get-tuple-element.358) | data formatting | bytes 1956864 | tf_op jit(solution)/shard_map/reshape | solution.py:208
  51.2 2.4 fusion.26
  53.6 10.6 %all-gather.2 = bf16[4,273,8]{1,2,0:T(8,128)(2,1)S(1)} all-gather(bf16[1,273,8]{1,2,0:T(8,128)(2,1)S(1)} %fusion.58), channel_id=3, replica_groups=mesh['req'=32,'seq'=4] {'seq'}, dimensions={0}, use_global_device_ids=true | all-gather | bytes 21840 | tf_op jit(solution)/shard_map/all_gather | solution.py:16
  65.1 2.1 fusion.59
  67.2 1.8 fusion.70
  69.3 3.3 %fusion.33 = f32[256,8,112]{0,2,1:T(8,128)} fusion(f32[256,8,112]{0,2,1:T(8,128)S(1)} %convolution_bitcast_fusion.2, f32[256,8]{0,1:T(8,128)S(1)} %get-tuple-element.359, f32[256,8,256]{0,2,1:T(8,128)S(1)} %bitcast.118, f32[256,8,16]{0,2,1:T(8,128)S(1)} %bitcast_convert_fusion.2, f32[273]{0:T(512)S(1)} %pad.3.clone), kind=kOutput, calls=%fused_computation.51 | convolution fusion | flops 753012736 | bytes 4072516 | tf_op jit(solution)/shard_map/while/body/eval_jaxpr/thf,fhv->thv/dot_general | solution.py:69
  72.6 11.0 %while.38 = (s32[]{:T(128)}, f32[273,896]{1,0:T(8,128)}, f32[273,8]{0,1:T(8,128)S(1)}, s32[]{:T(128)}, bf16[4,8]{1,0:T(4,128)(2,1)S(1)}, /*index=5*/bf16[4,273,8...) while((s32[]{:T(128)}, f32[273,896]{1,0:T(8,128)}, ...), condition=%wide.region_6.7_spmd.clone, body=%wide.region_5.6_spmd.clone.sunk | while | flops 1233972 | bytes 2482495 | solution.py:33
  72.8 2.2 fusion.91
  75.2 2.5 %fusion.91 = f32[273,896]{1,0:T(8,128)} fusion(f32[273,896]{1,0:T(8,128)} %get-tuple-element.454, bf16[4,273,896]{2,1,0:T(8,128)(2,1)} %get-tuple-element.467, s32[]{:T(128)} %get-tuple-element.453, f32[896]{0:T(1024)S(1)} %mul.567, pred[]{:T(512)S(6)} %compare.5, pred[]{:T(512)S(6)} %lt.65), kind=kLoop, calls=%fused_computation.1.clone.1 | loop fusion | flops 1223040 | bytes 2449670 | tf_op jit(solution)/shard_map/while/body/eval_jaxpr/jit(_where)/select_n | solution.py:31
  78.0 2.6 %fusion.91 = f32[273,896]{1,0:T(8,128)} fusion(f32[273,896]{1,0:T(8,128)} %get-tuple-element.454, bf16[4,273,896]{2,1,0:T(8,128)(2,1)} %get-tuple-element.467, s32[]{:T(128)} %get-tuple-element.453, f32[896]{0:T(1024)S(1)} %mul.567, pred[]{:T(512)S(6)} %compare.5, pred[]{:T(512)S(6)} %lt.65), kind=kLoop, calls=%fused_computation.1.clone.1 | loop fusion | flops 1223040 | bytes 2449670 | tf_op jit(solution)/shard_map/while/body/eval_jaxpr/jit(_where)/select_n | solution.py:31
  80.8 2.5 %fusion.91 = f32[273,896]{1,0:T(8,128)} fusion(f32[273,896]{1,0:T(8,128)} %get-tuple-element.454, bf16[4,273,896]{2,1,0:T(8,128)(2,1)} %get-tuple-element.467, s32[]{:T(128)} %get-tuple-element.453, f32[896]{0:T(1024)S(1)} %mul.567, pred[]{:T(512)S(6)} %compare.5, pred[]{:T(512)S(6)} %lt.65), kind=kLoop, calls=%fused_computation.1.clone.1 | loop fusion | flops 1223040 | bytes 2449670 | tf_op jit(solution)/shard_map/while/body/eval_jaxpr/jit(_where)/select_n | solution.py:31
  83.6 2.8 %reshape.198 = f32[273,8,112]{2,1,0:T(8,128)} reshape(f32[273,896]{1,0:T(8,128)} %get-tuple-element.291) | data formatting | bytes 1956864 | tf_op jit(solution)/shard_map/reshape | solution.py:230
  86.4 1.8 add_bitcast_fusion
  88.2 1.9 copy.47
  90.2 1.5 fusion.52
  91.8 3.0 %fusion.34 = bf16[256,8,112]{0,2,1:T(8,128)(2,1)S(1)} fusion(f32[256,8,112]{0,2,1:T(8,128)S(1)} %copy-done.9, f32[273,8,112]{2,1,0:T(8,128)S(1)} %copy-done.8, f32[256,8]{0,1:T(8,128)S(1)} %fusion.54, f32[256,8]{0,1:T(8,128)S(1)} %get-tuple-element.359, f32[256,8,256]{0,2,1:T(8,128)S(1)} %bitcast.120, f32[256,8,16]{0,2,1:T(8,128)S(1)} %bitcast_convert_fusion.2, ...), kind=kOutput, calls=%fused_computation.54 | convolution fusion | flops 753471488 | bytes 4600388 | tf_op jit(solution)/shard_map/thf,fhv->thv/dot_general | solution.py:227
  94.8 2.1 fusion.18
  96.9 0.7 fusion.51
  97.6 22.0 %all-gather.10.cloned.1.call-done = bf16[1792,1792]{0,1:T(8,128)(2,1)} async-done(((bf16[1792,56]{0,1:T(8,128)(2,1)}), bf16[1792,1792]{0,1:T(8,128)(2,1)}) %all-gather.10.cloned.1.call-update) | async-done | bytes 6422544 | tf_op jit(solution)/shard_map/all_gather | solution.py:121
  119.6 6.3 %fusion.49 = f32[256,1792]{1,0:T(8,128)} fusion(bf16[1792,1792]{0,1:T(8,128)(2,1)} %all-gather.10.cloned.1.call-done, bf16[256,1792]{1,0:T(8,128)(2,1)} %get-tuple-element.370, f32[1792]{0:T(1024)S(1)} %copy-done.26, f32[256]{0:T(256)S(1)} %add_rsqrt_fusion), kind=kOutput, calls=%fused_computation.75 | convolution fusion | flops 1646002176 | bytes 9183232 | tf_op jit(solution)/shard_map/while/body/dot_general | solution.py:126
  125.9 44.1 %all-gather.12.cloned.1.call-done = bf16[1792,1792]{0,1:T(8,128)(2,1)} async-done(((bf16[1792,56]{0,1:T(8,128)(2,1)}), bf16[1792,1792]{0,1:T(8,128)(2,1)}) %all-gather.12.cloned.1.call-update) | async-done | bytes 6422544 | tf_op jit(solution)/shard_map/all_gather | solution.py:122
  170.0 50.2 %all-gather.14.cloned.1.call-done = bf16[1792,1792]{0,1:T(8,128)(2,1)} async-done(((bf16[1792,56]{0,1:T(8,128)(2,1)}), bf16[1792,1792]{0,1:T(8,128)(2,1)}) %all-gather.14.cloned.1.call-update) | async-done | bytes 6422544 | tf_op jit(solution)/shard_map/all_gather | solution.py:123
  220.2 10.4 %fusion.45 = f32[256,1792]{1,0:T(8,128)} fusion(bf16[1792,1792]{0,1:T(8,128)(2,1)} %all-gather.14.cloned.1.call-done, bf16[1792,1792]{0,1:T(8,128)(2,1)} %all-gather.12.cloned.1.call-done, f32[256,1792]{1,0:T(8,128)} %fusion.49, bf16[256,1792]{1,0:T(8,128)(2,1)} %get-tuple-element.370, f32[1792]{0:T(1024)S(1)} %copy-done.26, f32[256]{0:T(256)S(1)} %add_rsqrt_fusion), kind=kOutput, calls=%fused_computation.72 | convolution fusion | flops 3292921856 | bytes 17440768 | tf_op jit(solution)/shard_map/while/body/dot_general | solution.py:129
  230.6 1.4 broadcast_in_dim.114
  232.0 3.5 %while.37 = (s32[]{:T(128)}, f32[256,1792]{1,0:T(8,128)}, s32[]{:T(128)}, f32[256,1792]{1,0:T(8,128)}, s32[]{:T(128)}) while((s32[]{:T(128)}, f32[256,1792]{1,0:T(8,128)}, s32[]{:T(128)}, f32[256,1792]{1,0:T(8,128)}, s32[]{:T(128)}) %tuple.84), condition=%wide.region_11.12_spmd, body=%wide.region_10.11_spmd.sunk | while | flops 458754 | bytes 5505085 | solution.py:134
  232.0 3.5 %add.275 = f32[256,1792]{1,0:T(8,128)} add(f32[256,1792]{1,0:T(8,128)} %get-tuple-element.477, f32[256,1792]{1,0:T(8,128)} %get-tuple-element.484) | non-fusion elementwise | flops 458752 | bytes 5505024 | tf_op jit(solution)/shard_map/while/body/add | solution.py:132
  235.5 2.9 %fusion.44 = bf16[1,256,1792]{2,1,0:T(8,128)(2,1)} fusion(f32[256,1792]{1,0:T(8,128)} %get-tuple-element.293, bf16[256,1792]{1,0:T(8,128)(2,1)} %get-tuple-element.370, f32[256]{0:T(256)S(1)} %copy-done.16), kind=kLoop, calls=%fused_computation.70 | loop fusion | flops 1835008 | bytes 3671040 | tf_op jit(solution)/shard_map/broadcast_in_dim | solution.py:251
  (108 shorter events, 4.4 us)
Async XLA Ops:
  7.2 87.6 %copy-start = (bf16[896,1792]{1,0:T(8,128)(2,1)S(1)}, bf16[896,1792]{1,0:T(8,128)(2,1)}, u32[]{:S(2)}) copy-start(bf16[896,1792]{1,0:T(8,128)(2,1)} %param.25) | copy-start | bytes 9633796
  7.2 8.7 %copy-start.19 = (f32[1,256,8]{1,2,0:T(8,128)S(1)}, f32[1,256,8]{1,2,0:T(8,128)}, u32[]{:S(2)}) copy-start(f32[1,256,8]{1,2,0:T(8,128)} %param.19) | copy-start | bytes 24580
  7.2 10.5 %copy-start.12 = (f32[3,1792]{1,0:T(4,128)S(1)}, f32[3,1792]{1,0:T(4,128)}, u32[]{:S(2)}) copy-start(f32[3,1792]{1,0:T(4,128)} %param.21) | copy-start | bytes 64516
  7.2 65.4 %all-gather.8.cloned.1.call-start = ((), (), s32[]{:S(2)}) async-start(), calls=%async_computation | async-start | bytes 2508800 | tf_op jit(solution)/shard_map/all_gather | solution.py:16
  10.3 0.9 copy-start.5
  11.3 6.5 %collective-permute-start = (bf16[2,1792]{1,0:T(2,128)(2,1)S(1)}, bf16[2,1792]{1,0:T(2,128)(2,1)S(1)}, u32[]{:S(2)}, u32[]{:S(2)}) collective-permute-start(bf16[2,1792]{1,0:T(2,128)(2,1)S(1)} %slice.39), channel_id=1, source_target_pairs={{0,1},{1,2},{2,3},{4,5},{5,6},{6,7},{8,9},{9,10},{10,11},{12,13},{... | collective-permute-start | bytes 21512 | tf_op jit(solution)/shard_map/ppermute | solution.py:10
  15.9 11.8 %copy-start.13 = (f32[256]{0:T(256)}, f32[256]{0:T(256)S(1)}, u32[]{:S(2)}) copy-start(f32[256]{0:T(256)S(1)} %get-tuple-element.371) | copy-start | bytes 3076
  16.8 3.9 %copy-start.10 = (bf16[1792,128]{1,0:T(8,128)(2,1)S(1)}, bf16[1792,128]{1,0:T(8,128)(2,1)}, u32[]{:S(2)}) copy-start(bf16[1792,128]{1,0:T(8,128)(2,1)} %param.23) | copy-start | bytes 1376260
  20.7 2.1 copy-start.3
  20.7 3.0 %copy-start.25 = (bf16[1792,896]{1,0:T(8,128)(2,1)S(1)}, bf16[1792,896]{1,0:T(8,128)(2,1)}, u32[]{:S(2)}) copy-start(bf16[1792,896]{1,0:T(8,128)(2,1)} %param.24) | copy-start | bytes 9633796
  30.9 7.3 %copy-start.28 = (u32[128]{0:T(128)S(1)}, u32[128]{0:T(128)}, u32[]{:S(2)}) copy-start(u32[128]{0:T(128)} %constant.124) | copy-start | bytes 1540
  32.4 18.7 %copy-start.14 = (f32[256]{0:T(256)S(1)}, f32[256]{0:T(256)}, u32[]{:S(2)}) copy-start(f32[256]{0:T(256)} %copy-done.13) | copy-start | bytes 3076
  34.8 84.8 %all-gather.10.cloned.1.call-start = ((), (), s32[]{:S(2)}) async-start(), calls=%async_computation.1 | async-start | bytes 6623232 | tf_op jit(solution)/shard_map/all_gather | solution.py:121
  35.6 134.4 %all-gather.12.cloned.1.call-start = ((), (), s32[]{:S(2)}) async-start(), calls=%async_computation.2 | async-start | bytes 6623232 | tf_op jit(solution)/shard_map/all_gather | solution.py:122
  36.3 183.9 %all-gather.14.cloned.1.call-start = ((), (), s32[]{:S(2)}) async-start(), calls=%async_computation.3 | async-start | bytes 6623232 | tf_op jit(solution)/shard_map/all_gather | solution.py:123
  39.5 14.1 %copy-start.23 = (f32[8]{0:T(128)}, f32[8]{0:T(128)S(1)}, u32[]{:S(2)}) copy-start(f32[8]{0:T(128)S(1)} %get-tuple-element.363) | copy-start | bytes 100
  48.4 5.1 %copy-start.21 = (f32[8]{0:T(128)S(1)}, f32[8]{0:T(128)}, u32[]{:S(2)}) copy-start(f32[8]{0:T(128)} %get-tuple-element.333) | copy-start | bytes 100
  51.1 13.1 %copy-start.4 = (bf16[256,1792]{1,0:T(8,128)(2,1)S(1)}, bf16[256,1792]{1,0:T(8,128)(2,1)}, u32[]{:S(2)}) copy-start(bf16[256,1792]{1,0:T(8,128)(2,1)} %copy-done.3) | copy-start | bytes 2752516
  51.1 13.1 %copy-start.11 = (bf16[1792,128]{1,0:T(8,128)(2,1)S(1)}, bf16[1792,128]{1,0:T(8,128)(2,1)}, u32[]{:S(2)}) copy-start(bf16[1792,128]{1,0:T(8,128)(2,1)} %param.22) | copy-start | bytes 1376260
  64.7 2.5 %copy-start.15 = (f32[256]{0:T(256)S(1)}, f32[256]{0:T(256)}, u32[]{:S(2)}) copy-start(f32[256]{0:T(256)} %copy-done.13) | copy-start | bytes 3076
  64.7 2.5 %copy-start.20 = (f32[8,256]{1,0:T(8,128)S(1)}, f32[8,256]{1,0:T(8,128)}, u32[]{:S(2)}) copy-start(f32[8,256]{1,0:T(8,128)} %add_bitcast_fusion.2) | copy-start | bytes 24580
  65.1 4.2 %copy-start.1 = (f32[256,8,16,16]{0,3,2,1:T(8,128)}, f32[256,8,16,16]{0,3,2,1:T(8,128)S(1)}, u32[]{:S(2)}) copy-start(f32[256,8,16,16]{0,3,2,1:T(8,128)S(1)} %multiply_multiply_fusion.2) | copy-start | bytes 6291460
  67.2 1.8 copy-start.7
  69.3 3.3 %copy-start.27 = (bf16[4,8]{1,0:T(4,128)(2,1)S(1)}, bf16[4,8]{1,0:T(4,128)(2,1)}, u32[]{:S(2)}) copy-start(bf16[4,8]{1,0:T(4,128)(2,1)} %reshape.203) | copy-start | bytes 196
  86.4 3.8 %copy-start.2 = (f32[256,8,16,16]{0,3,2,1:T(8,128)S(1)}, f32[256,8,16,16]{0,3,2,1:T(8,128)}, u32[]{:S(2)}) copy-start(f32[256,8,16,16]{0,3,2,1:T(8,128)} %copy-done.1) | copy-start | bytes 6291460
  88.2 3.5 %copy-start.17 = (f32[8,1,256]{2,1,0:T(1,128)S(1)}, f32[8,1,256]{2,1,0:T(1,128)}, u32[]{:S(2)}) copy-start(f32[8,1,256]{2,1,0:T(1,128)} %fusion.59) | copy-start | bytes 24580
  88.2 3.5 %copy-start.18 = (f32[8,256]{1,0:T(8,128)S(1)}, f32[8,256]{1,0:T(8,128)}, u32[]{:S(2)}) copy-start(f32[8,256]{1,0:T(8,128)} %get-tuple-element.367) | copy-start | bytes 24580
  88.2 3.5 %copy-start.8 = (f32[273,8,112]{2,1,0:T(8,128)S(1)}, f32[273,8,112]{2,1,0:T(8,128)}, u32[]{:S(2)}) copy-start(f32[273,8,112]{2,1,0:T(8,128)} %reshape.198) | copy-start | bytes 2935300
  88.2 3.5 %copy-start.9 = (f32[256,8,112]{0,2,1:T(8,128)S(1)}, f32[256,8,112]{0,2,1:T(8,128)}, u32[]{:S(2)}) copy-start(f32[256,8,112]{0,2,1:T(8,128)} %fusion.33) | copy-start | bytes 2752516
  91.7 3.0 %copy-start.6 = (bf16[1,256,1792]{2,1,0:T(8,128)(2,1)S(1)}, bf16[1,256,1792]{2,1,0:T(8,128)(2,1)}, u32[]{:S(2)}) copy-start(bf16[1,256,1792]{2,1,0:T(8,128)(2,1)} %param.17) | copy-start | bytes 2752516
  94.8 2.2 copy-start.22
  94.8 2.2 copy-start.24
  94.8 24.8 %copy-start.26 = (f32[1792]{0:T(1024)S(1)}, f32[1792]{0:T(1024)}, u32[]{:S(2)}) copy-start(f32[1792]{0:T(1024)} %param.26) | copy-start | bytes 21508
  232.0 3.5 %copy-start.16 = (f32[256]{0:T(256)S(1)}, f32[256]{0:T(256)}, u32[]{:S(2)}) copy-start(f32[256]{0:T(256)} %copy-done.13) | copy-start | bytes 3076
Sparse Core Ops, SparseCore 0:
  35.0 32.3 all-gather.7
  69.7 49.8 all-gather.9
  122.0 47.9 all-gather.11
  172.2 47.9 all-gather.13
where the time goes:
time: 246 us; the launch traced here: 245 us
  waiting for transfers between devices  118 us (48%)
  matrix products  36.9 us (15%)
  other arithmetic  33.8 us (14%)
  blocking collectives  17.8 us (7%)
  local copies, waits for them, and re-layouts  17.7 us (7%)
  between operations  16.2 us (7%)
  starting transfers between devices  4.09 us (2%)
    all_gather x1, waiting for transfers between devices, feed_forward(): down_piece = lax.all_gather(down_weight, 'req', axis=1, tiled=True)  50.2 us
    all_gather x1, waiting for transfers between devices, feed_forward(): up_piece = lax.all_gather(up_weight, 'req', axis=1, tiled=True)  44.1 us
    all_gather x1, waiting for transfers between devices, feed_forward(): gate_piece = lax.all_gather(gate_weight, 'req', axis=1, tiled=True)  22 us
    all_gather x1, blocking collectives, entering(): lax.all_gather(part.astype(kind), axis)  10.6 us
    dot_general x1, matrix products, add_block(): lax.dot_general(hidden_units, down_piece, (((1,), (1,)), ((), ())), prefe...  10.4 us
    select_n x8, other arithmetic, hop(): return jax.tree.map(lambda a, b: jnp.where(reached, a, b), new, before)  10.2 us
    unnamed x1, blocking collectives  7.18 us
    dot_general x1, matrix products, add_block(): gate_act = jnp.dot(row_data, gate_piece, preferred_element_type=jnp.float32)  6.26 us
  transfers between devices with their start and end apart: 5, of which 3 were waited for; matrix products, arithmetic and copies ran while one was open for 20% of the time, Pallas kernels for 0%

commit v1 on v0

v1 whole, which is shorter than its diff:
```python
import functools

import jax
import jax.numpy as jnp
import numpy as np
from jax import lax
from jax.experimental import pallas as pl
from jax.experimental.pallas import tpu as pltpu
from jax.sharding import PartitionSpec as P

MESH = pl.DeviceIdType.MESH
F32, BF16 = jnp.float32, jnp.bfloat16
D, HEADS, DV, FI, L, SH = 1792, 8, 112, 16, 256, 56
ROWS = 3 * SH + 8
NF = 160
HALF = D // 2
CUT = 96
GROUPS = 4
PER = HEADS // GROUPS


def expansion():
    e = np.zeros((1 + FI + FI * FI, NF), np.float32)
    e[0, 136] = 1
    for i in range(FI):
        e[1 + i, 144 + i] = 1
        for j in range(FI):
            a, d = i, (j - i) % FI
            if d > 8 or (d == 8 and i >= 8):
                a, d = j, (i - j) % FI
            e[17 + FI * i + j, 16 * d + a] = 1
    return e


def nt(a, b):
    return lax.dot_general(a, b, (((1,), (1,)), ((), ())), preferred_element_type=F32)


def nn(a, b):
    return jnp.dot(a, b, preferred_element_type=F32)


def rms(rows, gain):
    factor = lax.rsqrt(jnp.mean(rows * rows, axis=-1, keepdims=True) + 1e-05)
    return (rows * factor * gain).astype(BF16)


def kernel(
    h_ref, len_ref, ld_ref, mg_ref, cw_ref, wq_hbm, wk_hbm, wv_hbm, wo_hbm, pg_ref,
    g_ref, u_ref, d_ref, e_ref,
    out_ref, st_ref, nm_ref,
    G, wq, wk, wv, wo, halo, nbuf, gbuf, kn, qt, kt, vt, near, phiq, mloc, prior, msend,
    att, mt, ntr, cumt, cumn, fade, grow, mixed, mlp, acc,
    load_sem, send_sem, recv_sem, psend, precv, hsem, csend, crecv,
):
    req, seq = lax.axis_index("req"), lax.axis_index("seq")
    y, z, c = req // 8, (req // 2) % 4, req % 2

    def at(yy, zz, cc):
        return (yy * 4 + zz) * 2 + cc

    def near_z(k):
        return at(y, (z + k + 4) % 4, c)

    def near_y(k):
        return at((y + k + 4) % 4, z, c)

    partner = at(y, z, 1 - c)
    loads = [
        pltpu.make_async_copy(src, dst, load_sem.at[i])
        for i, (src, dst) in enumerate(((wq_hbm, wq), (wk_hbm, wk), (wv_hbm, wv), (wo_hbm, wo)))
    ]
    for load in loads:
        load.start()

    barrier = pltpu.get_barrier_semaphore()
    for r, s in (
        (near_z(1), seq), (near_z(-1), seq), (near_y(1), seq), (near_y(-1), seq),
        (partner, seq), (req, (seq + 1) % 4), (req, (seq + 3) % 4),
    ):
        pl.semaphore_signal(barrier, inc=1, device_id=(r, s), device_id_type=MESH)

    @pl.loop(0, 7)
    def _(j):
        cols = pl.ds(pl.multiple_of(j * 256, 256), 256)
        parts = [ref[:, cols].astype(F32) for ref in (g_ref, u_ref, d_ref)]
        parts.append(jnp.zeros((8, 256), F32))
        G[req, :, cols] = jnp.concatenate(parts, axis=0).astype(BF16)

    @pl.when(seq == 0)
    def _():
        prior[...] = jnp.zeros_like(prior)

    pl.semaphore_wait(barrier, 7)

    halo_copy = pltpu.make_async_remote_copy(
        h_ref.at[pl.ds(L - 16, 16)], halo, hsem.at[0], hsem.at[1],
        device_id=(req, (seq + 1) % 4), device_id_type=MESH,
    )

    @pl.when(seq < 3)
    def _():
        halo_copy.start()

    count = [0]
    started, waiting = [], {}

    def shard(part, a1, a2):
        yy, zz = (a2, a1) if part == 0 else (a1, a2)
        return at((y + yy + 4) % 4, (z + zz + 4) % 4, c)

    def to(part, axis, k):
        along_z = (part == 0) == (axis == 1)
        return near_z(k) if along_z else near_y(k)

    def region(slot, part, piece):
        cols = pl.ds(part * HALF, HALF)
        rows = (pl.ds(0, ROWS), pl.ds(0, CUT), pl.ds(CUT, ROWS - CUT))[piece]
        return G.at[slot, rows, cols]

    def send(key, part, axis, k, slot, piece, slot_in):
        n = count[0]
        count[0] += 1
        src = region(slot, part, piece)
        copy = pltpu.make_async_remote_copy(
            src, src, send_sem.at[n], recv_sem.at[n],
            device_id=(to(part, axis, k), seq), device_id_type=MESH,
        )
        copy.start()
        started.append(copy)
        dst = region(slot_in, part, piece)
        waiting[key] = pltpu.make_async_remote_copy(
            dst, dst, send_sem.at[n], recv_sem.at[n],
            device_id=(to(part, axis, k), seq), device_id_type=MESH,
        )

    pcount = [0]
    pwaiting = {}

    def other(slot):
        return slot + 1 - 2 * c

    def share(key, part, slot):
        n = pcount[0]
        pcount[0] += 1
        src, dst = region(slot, part, 0), region(other(slot), part, 0)
        copy = pltpu.make_async_remote_copy(
            src, src, psend.at[n], precv.at[n], device_id=(partner, seq), device_id_type=MESH
        )
        copy.start()
        started.append(copy)
        pwaiting[key] = pltpu.make_async_remote_copy(
            dst, dst, psend.at[n], precv.at[n], device_id=(partner, seq), device_id_type=MESH
        )

    OFF = (0, -1, 1, 2)

    def first(part):
        for k in (1, -1):
            send(("p1", part, k), part, 1, k, shard(part, 0, 0), 0, shard(part, -k, 0))

    def second(part, j):
        a1 = OFF[j]
        for k in (1, -1):
            send(("q1", part, j, k), part, 2, k, shard(part, a1, 0), 0, shard(part, a1, -k))

    def forward_first(part):
        for k in (1, -1):
            waiting[("p1", part, k)].wait_recv()
            piece = 1 if k == 1 else 2
            send(("p2", part, k), part, 1, k, shard(part, -k, 0), piece, shard(part, 2, 0))

    def forward_second(part, j):
        a1 = OFF[j]
        for k in (1, -1):
            waiting[("q1", part, j, k)].wait_recv()
            piece = 2 if k == 1 else 1
            send(("q2", part, j, k), part, 2, k, shard(part, a1, -k), piece, shard(part, a1, 2))
        for k in (1, -1):
            share((part, a1, -k), part, shard(part, a1, -k))

    def finish_second(part, j):
        for k in (1, -1):
            waiting[("q2", part, j, k)].wait_recv()
        share((part, OFF[j], 2), part, shard(part, OFF[j], 2))

    def service(point):
        both = (0, 1)
        if point == 0:
            for part in both:
                first(part)
            for part in both:
                second(part, 0)
            for part in both:
                share((part, 0, 0), part, shard(part, 0, 0))
        if point == 1:
            for part in both:
                forward_first(part)
            for j in (1, 2):
                for part in both:
                    second(part, j)
            for part in both:
                for k in (1, -1):
                    share((part, -k, 0), part, shard(part, -k, 0))
        if point == 2:
            for part in both:
                for k in (1, -1):
                    waiting[("p2", part, k)].wait_recv()
                second(part, 3)
                share((part, 2, 0), part, shard(part, 2, 0))
            for part in both:
                forward_second(part, 0)
        if point == 3:
            for j in (1, 2):
                for part in both:
                    forward_second(part, j)
        if point == 4:
            for part in both:
                forward_second(part, 3)
            for part in both:
                finish_second(part, 0)
        if point == 5:
            for j in (1, 2):
                for part in both:
                    finish_second(part, j)
        if point == 6:
            for part in both:
                finish_second(part, 3)

    def arrived(*keys):
        for dy, dz in keys:
            pwaiting[(0, dz, dy)].wait_recv()
            pwaiting[(1, dy, dz)].wait_recv()

    service(0)

    @pl.loop(0, 8)
    def _(b):
        rows = pl.ds(pl.multiple_of(b * 32, 32), 32)
        block = rms(h_ref[rows, :].astype(F32), mg_ref[...])
        nbuf[pl.ds(pl.multiple_of(b * 32 + 8, 8), 32), :] = block.astype(F32)

    length = len_ref[0] - seq * L
    valid_row = lax.broadcasted_iota(jnp.int32, (1, L), 1) < length
    valid_col = lax.broadcasted_iota(jnp.int32, (L, 1), 0) < length
    rate = jnp.where(valid_row, ld_ref[...], 0.0)
    upper = lax.broadcasted_iota(jnp.int32, (L, L), 0) <= lax.broadcasted_iota(jnp.int32, (L, L), 1)
    cum = jnp.dot(
        rate, upper.astype(F32), precision=lax.Precision.HIGHEST, preferred_element_type=F32
    )
    cumn[...] = cum.T
    closing = cum[:, L - 1 :]
    fades = jnp.where(valid_row, jnp.exp(closing - cum), 0.0)
    grows = jnp.exp(cum)
    for h in range(HEADS):
        cumt[h] = cum[h : h + 1]
        fade[h] = fades[h : h + 1]
        grow[h] = grows[h : h + 1]

    @pl.when(seq == 0)
    def _():
        nbuf[pl.ds(0, 8), :] = jnp.zeros((8, D), F32)

    @pl.when(seq > 0)
    def _():
        halo_copy.wait_recv()
        block = rms(halo[...].astype(F32), mg_ref[...]).astype(F32)
        nbuf[pl.ds(0, 8), :] = block[8:16]

    @pl.loop(0, 8)
    def _(b):
        rows = pl.ds(pl.multiple_of(b * 32, 32), 32)
        block = nbuf[pl.ds(pl.multiple_of(b * 32, 8), 40), :]
        here = block[8:40]
        conv = cw_ref[0:1] * here + cw_ref[1:2] * block[7:39] + cw_ref[2:3] * block[6:38]
        gbuf[rows, :] = (conv * jax.nn.sigmoid(here)).astype(BF16)

    loads[0].wait()
    loads[1].wait()
    qn = (nn(gbuf[...], wq[...]) * 0.5).astype(BF16)
    keys = (nn(gbuf[...], wk[...]) * 0.5).astype(BF16)
    kn[...] = keys
    qt[...] = qn.astype(F32).T
    kt[...] = keys.astype(F32).T
    loads[2].wait()

    @pl.loop(0, 2)
    def _(b):
        rows = pl.ds(pl.multiple_of(b * 128, 128), 128)
        values = nn(gbuf[rows, :], wv[...])
        turned = values.T.astype(BF16)
        for h in range(HEADS):
            vt[h, 0:DV, rows] = turned[h * DV : (h + 1) * DV]

    ones = (lax.broadcasted_iota(jnp.int32, (16, L), 0) == 0).astype(BF16)
    for h in range(HEADS):
        vt[h, DV:128, :] = ones

    service(1)

    row16 = lax.broadcasted_iota(jnp.int32, (16, L), 0)
    lane128 = lax.broadcasted_iota(jnp.int32, (L, 128), 1)

    def phi(x, w, middle, square):
        parts = [x * w * square]
        for d in range(1, 9):
            parts.append(w * pltpu.roll(x, 16 - d, 0))
        parts[0] = square * (w * x)
        parts[8] = jnp.where(row16 < 8, parts[8], jnp.where(row16 == 8, middle, 0.0))
        parts.append(w)
        return jnp.concatenate(parts, axis=0).astype(BF16)

    @pl.loop(0, HEADS)
    def _(h):
        head = pl.ds(pl.multiple_of(h * 16, 16), 16)
        k_h, q_h = kt[head, :], qt[head, :]
        k_only = jnp.where(lane128 // 16 == h, kn[...], jnp.zeros_like(kn))
        scores = nn(k_only, qt[...].astype(BF16))
        lane8 = lax.broadcasted_iota(jnp.int32, (L, HEADS), 1)
        col = jnp.sum(jnp.where(lane8 == h, cumn[...], 0.0), axis=1, keepdims=True)
        gap = jnp.minimum(cumt[h] - col, 0.0)
        causal = lax.broadcasted_iota(jnp.int32, (L, L), 0) <= lax.broadcasted_iota(
            jnp.int32, (L, L), 1
        )
        weights = jnp.where(causal, jnp.exp(gap), 0.0) * ((0.5 * scores + 1.0) * scores + 1.0)
        near[h] = nn(vt[h], weights.astype(BF16))
        f_h, g_h = fade[h], grow[h]
        mloc[h] = nt(phi(k_h, k_h * f_h, jnp.broadcast_to(f_h, (16, L)), 1.0), vt[h])
        phiq[h] = phi(q_h, q_h * g_h, jnp.broadcast_to(g_h, (16, L)), 0.5)

    service(2)

    for g in range(GROUPS):
        heads = pl.ds(g * PER, PER)
        chain = pltpu.make_async_remote_copy(
            msend.at[heads], prior.at[heads], csend.at[g], crecv.at[g],
            device_id=(req, (seq + 1) % 4), device_id_type=MESH,
        )

        @pl.when(seq > 0)
        def _():
            chain.wait_recv()

        for h in range(g * PER, (g + 1) * PER):
            end = prior[h].astype(F32) * grow[h][:, L - 1 :] + mloc[h]
            mloc[h] = end
            msend[h] = end.astype(BF16)

        @pl.when(seq < 3)
        def _():
            chain.start()

    @pl.loop(0, HEADS)
    def _(h):
        before = prior[h].astype(F32).T.astype(BF16)
        numer = near[h] + nn(before, phiq[h])
        rows = pl.ds(pl.multiple_of(h * DV, 16), DV)
        att[rows, :] = (numer[0:DV] / numer[DV : DV + 1]).astype(BF16)
        turned = mloc[h].T
        mt[rows, :] = turned[0:DV]
        ntr[pl.ds(h, 1), :] = turned[DV : DV + 1]

    loads[3].wait()
    attended = att[...].astype(F32).T.astype(BF16)
    mixed[...] = (h_ref[...].astype(F32) + nn(attended, wo[...])).astype(BF16)

    @pl.loop(0, 8)
    def _(b):
        rows = pl.ds(pl.multiple_of(b * 32, 32), 32)
        mlp[rows, :] = rms(mixed[rows, :].astype(F32), pg_ref[...])

    service(3)

    def pair(first_chip, second_chip, start=False):
        bases = [at((y + dy + 4) % 4, (z + dz + 4) % 4, 0) for dy, dz in (first_chip, second_chip)]
        turned = []
        for base in bases:
            weights = G[pl.ds(base, 2), 0 : 2 * SH, :].reshape(4 * SH, D)
            both = nt(weights, mlp[...])
            for s in range(2):
                gate = both[s * 2 * SH : s * 2 * SH + SH]
                up = both[s * 2 * SH + SH : (s + 1) * 2 * SH]
                turned += [jax.nn.silu(gate) * up, jnp.zeros((8, L), F32)]
        hidden = jnp.concatenate(turned, axis=0).T.astype(BF16)
        total = nn(hidden[:, 0:128], G[pl.ds(bases[0], 2), 2 * SH : ROWS, :].reshape(128, D))
        total += nn(hidden[:, 128:256], G[pl.ds(bases[1], 2), 2 * SH : ROWS, :].reshape(128, D))
        acc[...] = total if start else acc[...] + total

    arrived((0, 0), (0, 1), (0, -1), (1, 0), (-1, 0))
    pair((0, 1), (0, -1), start=True)
    pair((1, 0), (-1, 0))

    e = e_ref[...]
    states = mt[...]
    high = states.astype(BF16)
    low = (states - high.astype(F32)).astype(BF16)
    row = lax.broadcasted_iota(jnp.int32, (273, 1), 0)
    scale = jnp.where(row < 17, 1.0, 0.5**0.5)
    st_ref[...] = (nt(e, high) + nt(e, low)) * scale
    sums = ntr[...]
    high = sums.astype(BF16)
    low = (sums - high.astype(F32)).astype(BF16)
    lane = lax.broadcasted_iota(jnp.int32, (1, 273), 1)
    nm_ref[...] = (nt(high, e) + nt(low, e)) * jnp.where(lane < 17, 1.0, 0.5**0.5)

    arrived((1, 1), (1, -1), (-1, 1), (-1, -1))
    pair((1, 1), (1, -1))
    pair((-1, 1), (-1, -1))
    service(4)
    arrived((2, 0), (0, 2))
    pair((2, 0), (0, 2))
    service(5)
    arrived((1, 2), (-1, 2), (2, 1), (2, -1))
    pair((1, 2), (-1, 2))
    pair((2, 1), (2, -1))
    service(6)
    arrived((2, 2))
    pair((0, 0), (2, 2))
    out_ref[...] = jnp.where(valid_col, mixed[...].astype(F32) + acc[...], 0.0).astype(BF16)

    for copy in started:
        copy.wait_send()

    @pl.when(seq < 3)
    def _():
        halo_copy.wait_send()
        for g in range(GROUPS):
            heads = pl.ds(g * PER, PER)
            pltpu.make_async_remote_copy(
                msend.at[heads], prior.at[heads], csend.at[g], crecv.at[g],
                device_id=(req, (seq + 1) % 4), device_id_type=MESH,
            ).wait_send()


def local(
    hidden_in, lengths, log_decay, mix_gain, conv_weight, query_weight, key_weight, value_weight,
    out_weight, mlp_gain, gate_weight, up_weight, down_weight,
):
    vmem = pl.BlockSpec(memory_space=pltpu.VMEM)
    smem = pl.BlockSpec(memory_space=pltpu.SMEM)
    anywhere = pl.BlockSpec(memory_space=pl.ANY)
    dma = pltpu.SemaphoreType.DMA
    result, states, norms = pl.pallas_call(
        kernel,
        name="layer",
        out_shape=(
            jax.ShapeDtypeStruct((L, D), BF16),
            jax.ShapeDtypeStruct((273, HEADS * DV), F32),
            jax.ShapeDtypeStruct((HEADS, 273), F32),
        ),
        in_specs=[vmem, smem, vmem, vmem, vmem] + [anywhere] * 4 + [vmem] * 5,
        out_specs=(vmem, vmem, vmem),
        scratch_shapes=[
            pltpu.VMEM((32, ROWS, D), BF16),
            pltpu.VMEM((D, 128), BF16),
            pltpu.VMEM((D, 128), BF16),
            pltpu.VMEM((D, HEADS * DV), BF16),
            pltpu.VMEM((HEADS * DV, D), BF16),
            pltpu.VMEM((16, D), BF16),
            pltpu.VMEM((L + 8, D), F32),
            pltpu.VMEM((L, D), BF16),
            pltpu.VMEM((L, 128), BF16),
            pltpu.VMEM((128, L), F32),
            pltpu.VMEM((128, L), F32),
            pltpu.VMEM((HEADS, 128, L), BF16),
            pltpu.VMEM((HEADS, 128, L), F32),
            pltpu.VMEM((HEADS, NF, L), BF16),
            pltpu.VMEM((HEADS, NF, 128), F32),
            pltpu.VMEM((HEADS, NF, 128), BF16),
            pltpu.VMEM((HEADS, NF, 128), BF16),
            pltpu.VMEM((HEADS * DV, L), BF16),
            pltpu.VMEM((HEADS * DV, NF), F32),
            pltpu.VMEM((HEADS, NF), F32),
            pltpu.VMEM((HEADS, 1, L), F32),
            pltpu.VMEM((L, HEADS), F32),
            pltpu.VMEM((HEADS, 1, L), F32),
            pltpu.VMEM((HEADS, 1, L), F32),
            pltpu.VMEM((L, D), BF16),
            pltpu.VMEM((L, D), BF16),
            pltpu.VMEM((L, D), F32),
            dma((4,)),
            dma((40,)),
            dma((40,)),
            dma((32,)),
            dma((32,)),
            dma((2,)),
            dma((GROUPS,)),
            dma((GROUPS,)),
        ],
        compiler_params=pltpu.CompilerParams(
            collective_id=0, has_side_effects=True, vmem_limit_bytes=63 * 1024 * 1024
        ),
    )(
        hidden_in[0], lengths, log_decay[0].T, mix_gain[None], conv_weight, query_weight,
        key_weight, value_weight, out_weight, mlp_gain[None], gate_weight.T, up_weight.T,
        down_weight.T, jnp.asarray(expansion(), BF16),
    )
    return (result[None], states[None, None], norms.T[None, None])


def solution(mesh):
    return jax.shard_map(
        local,
        mesh=mesh,
        in_specs=(
            P("req", "seq", None),
            P("req"),
            P("req", "seq", None),
            P(),
            P(),
            P(),
            P(),
            P(),
            P(),
            P(),
            P(None, "req"),
            P(None, "req"),
            P(None, "req"),
        ),
        out_specs=(P("req", "seq", None), P("req", "seq", None, None), P("req", "seq", None, None)),
        check_vma=False,
    )
```

time: 246 us -> 79.7 us (0.32)
  the two profiles are of different devices: /device:TPU:1 before, /device:TPU:6 now
where the time goes in v1:
time: 79.7 us; the launch traced here: 79.4 us
  Pallas kernels  69.5 us (87%)
  local copies, waits for them, and re-layouts  8.52 us (11%)
  between operations  1.3 us (2%)
    pallas_call x1, Pallas kernels, local(): pl.pallas_call(kernel, name='layer', out_shape=(jax.ShapeDtypeStruct((L,...  69.5 us
    unnamed x5, local copies, waits for them, and re-layouts  5.93 us

profile of v1, /device:TPU:6, one launch (start us, length us, event | category | flops | bytes accessed | tf_op | source)
XLA Modules:
  0.0 79.4 jit_solution(17788352115514207875)
XLA Ops:
  1.3 1.3 %broadcast_in_dim.15.mg_ref = f32[1,1792]{1,0:T(1,128)} reshape(f32[1792]{0:T(1024)} %param.17) | data formatting | bytes 14336 | tf_op jit(solution)/shard_map/broadcast_in_dim | solution.py:494
  2.6 1.3 %broadcast_in_dim.16.pg_ref = f32[1,1792]{1,0:T(1,128)} reshape(f32[1792]{0:T(1024)} %param.23) | data formatting | bytes 14336 | tf_op jit(solution)/shard_map/broadcast_in_dim | solution.py:495
  3.9 69.5 %layer.1 = (bf16[256,1792]{1,0:T(8,128)(2,1)}, f32[273,896]{1,0:T(8,128)}, f32[8,273]{1,0:T(8,128)}) custom-call(bf16[256,1792]{1,0:T(8,128)(2,1)} %bitcast.13, s32[1]{0:T(128)S(6)} %copy.20.len_ref, f32[8,256]{1,0:T(8,128)} %bitcast.19, f32[1,1792]{1,0:T(1,128)} %broadcast_in_dim.15.mg_ref, f32[3,1792]{1,0:T(4,128)} %cw_ref.1, bf16[1792,128]{1,0:T(8,128)(2,1)} %wq_hbm.1, ...), custom_call_target="tpu_custom_call" | custom-call | tf_op jit(solution)/shard_map/layer/pallas_call | solution.py:443
  73.4 0.0 copy-start
  73.4 3.2 %copy.17 = f32[1,1,273,896]{3,1,2,0:T(1,128)} copy(f32[1,1,273,896]{3,2,1,0:T(8,128)} %bitcast.12) | data formatting | bytes 1956864
  76.6 2.2 %copy.21 = bf16[1,256,1792]{2,1,0:T(8,128)(2,1)} copy(bf16[1,256,1792]{2,1,0:T(8,128)(2,1)} %bitcast.14) | data formatting | bytes 1835008
  78.8 0.0 copy-done
  78.8 0.6 copy.22
Async XLA Ops:
  73.4 5.3 %copy-start = (f32[8,273]{1,0:T(8,128)S(1)}, f32[8,273]{1,0:T(8,128)}, u32[]{:S(2)}) copy-start(f32[8,273]{1,0:T(8,128)} %get-tuple-element.8) | copy-start | bytes 26212
